TPU v7x, 32 devices: a whole 2x2x4 slice. The times are simulated.
32 devices in a mesh: groups: 2 (over x), seq: 16 (over z, y, core).
Axes of the slice: x: 2, y: 2, z: 4, core: 2. Of those that a mesh axis runs over, the one named last changes fastest.
Arguments:
- queries: bfloat16 [96, 8192], P(('groups', 'seq')), parts along dimension 0, may hold values from -9 to 9, as said below
- key_rows: bfloat16 [8192, 8192], P(('groups', 'seq')), parts along dimension 0, may hold values from -9 to 9, as said below
- value_rows: bfloat16 [8192, 8192], P(('groups', 'seq')), parts along dimension 0, may hold values from -6 to 6
- out_weight: bfloat16 [8192, 4096], P('seq'), may hold values from -6 to 6
- levels: int32 [3, 96], P(None, ('groups', 'seq')), parts along dimension 1, may hold values from 0 to 8
- owner_map: int32 [3, 96], P(None, ('groups', 'seq')), parts along dimension 1, may hold values from 0 to 47, each once within a row
Outputs:
- base_update: bfloat16 [96, 4096], P(('groups', 'seq')), parts along dimension 0
There are 2 independent parts, one for each index of `groups`. A program takes and returns all parts, laid end to end along the dimension named above; an argument that names none is the same for every part. Nothing has to cross between parts.
Inputs may be any that keep to these rules, and one draw needn't show every extreme that they name: queries: of order one, a few entries larger. key_rows: of order one, a few entries larger. Each row of owner_map names every base query token once; it stands in for a resampling onto base positions.
All inputs are finite; a program needn't handle non-finite values.
Results may differ from a plain program's by a relative error of at most 0.02.
Values may be sent and summed in bfloat16 or wider, within the bound.
No kernel may reach another device: no remote copies, remote signals or barrier semaphores. Data moves between devices by JAX's collectives and lax.ppermute only.
A program may use at most 128 MiB of HBM per device.

v0:
```python
import jax
import jax.numpy as jnp
from jax import lax
from jax.sharding import PartitionSpec as P

HD = 128
HEADS = 16
CONTROLS = 3
LEVELS = 8


def local_block(operands):
    query_block, key_block, value_block = operands
    scores = jnp.einsum(
        "qph,kph->pqk", query_block, key_block, preferred_element_type=jnp.float32
    ) * HD ** (-0.5)
    peak = jnp.max(scores, axis=2)
    expo = jnp.exp(scores - peak[:, :, None])
    total = jnp.sum(expo, axis=2)
    weighted = jnp.einsum(
        "pqk,kph->pqh", expo.astype(jnp.bfloat16), value_block, preferred_element_type=jnp.float32
    )
    return (weighted, peak, total)


def on_device(queries, key_rows, value_rows, out_weight, levels, owner_map):
    seq_count = lax.axis_size("seq")
    query_dev = queries.shape[0]
    total_queries = query_dev * seq_count
    pairs = queries.shape[1] // HD
    heads_dev = out_weight.shape[0] // HD
    level_all, owner_all = (
        lax.all_gather(levels, "seq", axis=1, tiled=True),
        lax.all_gather(owner_map, "seq", axis=1, tiled=True),
    )
    gathered = lax.all_gather(queries, "seq", axis=0, tiled=True)
    blocks = pairs // 8
    query_split = gathered.reshape(total_queries, blocks, 8, HD).transpose(1, 0, 2, 3)
    key_split = key_rows.reshape(-1, blocks, 8, HD).transpose(1, 0, 2, 3)
    value_split = value_rows.reshape(-1, blocks, 8, HD).transpose(1, 0, 2, 3)
    weighted, peak, total = lax.map(local_block, (query_split, key_split, value_split))
    weighted = weighted.reshape(pairs, total_queries, HD)
    peak = peak.reshape(pairs, total_queries)
    total = total.reshape(pairs, total_queries)
    part_out, part_peak, part_total = (
        lax.all_to_all(
            weighted[:, None].astype(jnp.bfloat16), "seq", split_axis=0, concat_axis=1, tiled=True
        ).astype(jnp.float32),
        lax.all_to_all(
            peak[:, None].astype(jnp.bfloat16), "seq", split_axis=0, concat_axis=1, tiled=True
        ).astype(jnp.float32),
        lax.all_to_all(
            total[:, None].astype(jnp.bfloat16), "seq", split_axis=0, concat_axis=1, tiled=True
        ).astype(jnp.float32),
    )
    best = jnp.max(part_peak, axis=1)
    factor = jnp.exp(part_peak - best[:, None])
    numer = jnp.sum(factor[..., None] * part_out, axis=1)
    denom = jnp.sum(factor * part_total, axis=1)
    attended = (numer / denom[..., None]).astype(jnp.bfloat16)
    section = lax.axis_index("seq") * heads_dev // HEADS
    is_base = section >= CONTROLS
    control = jnp.minimum(section, CONTROLS - 1)
    owner_here = lax.dynamic_index_in_dim(owner_all, control, 0, keepdims=False)
    level_here = lax.dynamic_index_in_dim(level_all, control, 0, keepdims=False)
    positions = jnp.arange(total_queries, dtype=jnp.int32)
    owner_here = jnp.where(is_base, positions, owner_here)
    level_here = jnp.where(is_base, LEVELS, level_here)
    selector = owner_here[None, :] == positions[:, None]
    chosen = jnp.einsum(
        "bt,pth->bph", selector.astype(jnp.bfloat16), attended, preferred_element_type=jnp.float32
    ).astype(jnp.bfloat16)
    mixed = chosen.reshape(total_queries, heads_dev * HD)
    row_weight = jnp.dot(selector.astype(jnp.float32), level_here.astype(jnp.float32)) / LEVELS
    summed = lax.psum_scatter(
        jnp.dot(mixed, out_weight, preferred_element_type=jnp.float32) * row_weight[:, None],
        "seq",
        scatter_dimension=0,
        tiled=True,
    )
    return summed.astype(jnp.bfloat16)


def solution(mesh):
    return jax.shard_map(
        on_device,
        mesh=mesh,
        in_specs=(
            P(("groups", "seq"), None),
            P(("groups", "seq"), None),
            P(("groups", "seq"), None),
            P("seq", None),
            P(None, ("groups", "seq")),
            P(None, ("groups", "seq")),
        ),
        out_specs=P(("groups", "seq"), None),
        check_vma=False,
    )
```

profile of v0, /device:TPU:0, one launch (start us, length us, event | category | flops | bytes accessed | tf_op | source)
XLA Modules:
  0.0 215.2 jit_solution(13509341424326010347)
XLA Ops:
  0.0 26.4 %all-gather.1 = bf16[16,3,8192]{2,1,0:T(4,128)(2,1)S(1)} all-gather(bf16[1,3,8192]{2,1,0:T(4,128)(2,1)} %bitcast.100), channel_id=1, replica_groups=mesh['groups'=2,'seq'=16] {'seq'}, dimensions={0}, use_global_device_ids=true | all-gather | bytes 835584 | tf_op jit(solution)/shard_map/all_gather | solution.py:36
  26.4 1.1 reshape.79
  27.5 6.4 %copy.33 = bf16[256,8192]{0,1:T(8,128)(2,1)} copy(bf16[256,8192]{1,0:T(8,128)(2,1)} %param.9) | data formatting | bytes 8388608 | tf_op args[1]
  33.9 6.4 %copy.34 = bf16[256,8192]{0,1:T(8,128)(2,1)} copy(bf16[256,8192]{1,0:T(8,128)(2,1)} %param.10) | data formatting | bytes 8388608 | tf_op args[2]
  40.3 0.0 copy-start
  40.3 0.0 copy-start.1
  40.3 0.0 copy-start.2
  40.3 29.4 %while.14 = (s32[]{:T(128)}, bf16[8,8,48,128]{3,2,1,0:T(8,128)(2,1)}, bf16[8,8,48]{2,1,0:T(8,128)(2,1)S(1)}, bf16[8,8,48]{2,1,0:T(8,128)(2,1)S(1)}, bf16[8,48,8,...) while((s32[]{:T(128)}, ...), condition=%wide.region_3.4_spmd, body=%wide.region_0.3_spmd.sunk | while | flops 50920704 | bytes 2738541 | solution.py:41
  40.3 1.3 fusion.35
  41.7 2.0 fusion.36
  43.7 0.2 fusion.37
  44.0 1.3 fusion.35
  45.4 2.0 fusion.36
  47.4 0.2 fusion.37
  47.7 1.3 fusion.35
  49.0 2.0 fusion.36
  51.1 0.2 fusion.37
  51.4 1.3 fusion.35
  52.7 2.0 fusion.36
  54.7 0.2 fusion.37
  55.0 1.3 fusion.35
  56.4 2.0 fusion.36
  58.4 0.2 fusion.37
  58.7 1.3 fusion.35
  60.1 2.0 fusion.36
  62.1 0.2 fusion.37
  62.4 1.3 fusion.35
  63.7 2.0 fusion.36
  65.8 0.2 fusion.37
  66.1 1.3 fusion.35
  67.4 2.0 fusion.36
  69.4 0.2 fusion.37
  69.7 0.6 copy.39
  70.3 3.5 %all-to-all-start.2 = ((bf16[64,1,48]{2,1,0:T(2,128)(2,1)}), bf16[64,1,48]{2,1,0:T(2,128)(2,1)S(1)}, u32[]{:S(2)}, u32[]{:S(2)}) async-start(bf16[64,1,48]{2,1,0:T(2,128)(2,1)} %copy.39), calls=%async_computation.2 | async-start | bytes 65536 | tf_op jit(solution)/shard_map/all_to_all | solution.py:52
  73.9 6.6 %all-to-all-done.2 = bf16[64,1,48]{2,1,0:T(2,128)(2,1)S(1)} async-done(((bf16[64,1,48]{2,1,0:T(2,128)(2,1)}), bf16[64,1,48]{2,1,0:T(2,128)(2,1)S(1)}, u32[]{:S(2)}, u32[]{:S(2)}) %all-to-all-start.2) | async-done | bytes 6176 | tf_op jit(solution)/shard_map/all_to_all | solution.py:52
  80.4 9.2 %all_to_all.33 = bf16[64,1,48]{2,1,0:T(2,128)(2,1)S(1)} all-to-all(bf16[64,1,48]{2,1,0:T(2,128)(2,1)S(1)} %copy.38), channel_id=1, replica_groups=mesh['groups'=2,'seq'=16] {'seq'}, dimensions={0} | all-to-all | bytes 12288 | tf_op jit(solution)/shard_map/all_to_all | solution.py:49
  89.6 3.6 %all-to-all-start.1 = ((bf16[64,1,48,128]{3,2,1,0:T(8,128)(2,1)}), bf16[64,1,48,128]{3,2,1,0:T(8,128)(2,1)S(1)}, u32[]{:S(2)}, u32[]{:S(2)}) async-start(bf16[64,1,48,128]{3,2,1,0:T(8,128)(2,1)} %bitcast.20), calls=%async_computation.1 | async-start | bytes 1572864 | tf_op jit(solution)/shard_map/all_to_all | solution.py:46
  93.3 0.0 copy-done
  93.3 0.1 copy.41
  93.4 29.1 %all-gather.2 = s32[16,3,3]{2,1,0:T(4,128)S(1)} all-gather(s32[1,3,3]{2,1,0:T(4,128)S(1)} %bitcast.103), channel_id=1, replica_groups=mesh['groups'=2,'seq'=16] {'seq'}, dimensions={0}, use_global_device_ids=true | all-gather | bytes 612 | tf_op jit(solution)/shard_map/all_gather | solution.py:33
  122.5 0.0 copy-done.1
  122.5 0.1 copy.31
  122.6 20.1 %all-gather = s32[16,3,3]{2,1,0:T(4,128)S(1)} all-gather(s32[1,3,3]{2,1,0:T(4,128)S(1)} %bitcast.104), channel_id=1, replica_groups=mesh['groups'=2,'seq'=16] {'seq'}, dimensions={0}, use_global_device_ids=true | all-gather | bytes 612 | tf_op jit(solution)/shard_map/all_gather | solution.py:34
  142.8 0.1 constant_dynamic-slice_fusion.1
  142.8 0.1 copy.49
  142.9 0.1 copy.50
  143.0 0.0 copy-done.2
  143.0 0.6 dynamic-slice.2
  144.3 0.1 fusion.13
  144.5 0.0 all-to-all-done.1
  144.5 0.5 fusion.11
  145.0 0.2 fusion.12
  145.2 3.0 %convolution_multiply_fusion.1 = f32[48,4096]{1,0:T(8,128)S(1)} fusion(bf16[512,4096]{1,0:T(8,128)(2,1)} %param.11, f32[48]{0:T(128)S(1)} %fusion.13, bf16[4,6,8,128]{3,2,1,0:T(8,128)(2,1)S(1)} %fusion.12), kind=kOutput, calls=%fused_computation.17 | convolution fusion | flops 201523200 | bytes 5030080 | tf_op jit(solution)/shard_map/dot_general | solution.py:76
  148.3 66.3 %all-reduce.2 = bf16[48,4096]{1,0:T(8,128)(2,1)S(1)} all-reduce(f32[48,4096]{1,0:T(8,128)S(1)} %convolution_multiply_fusion.1), channel_id=2, replica_groups=mesh['groups'=2,'seq'=16] {'seq'}, use_global_device_ids=true, to_apply=%region_7.8.clone | all-reduce | flops 196608 | bytes 1179648
  214.6 0.6 dynamic-slice_convert_fusion
  (36 shorter events, 0.6 us)
Async XLA Ops:
  40.3 53.0 %copy-start = (s32[3,3]{1,0:T(4,128)S(1)}, s32[3,3]{1,0:T(4,128)}, u32[]{:S(2)}) copy-start(s32[3,3]{1,0:T(4,128)} %param.12) | copy-start | bytes 112
  40.3 82.2 %copy-start.1 = (s32[3,3]{1,0:T(4,128)S(1)}, s32[3,3]{1,0:T(4,128)}, u32[]{:S(2)}) copy-start(s32[3,3]{1,0:T(4,128)} %param.13) | copy-start | bytes 112
  40.3 102.7 %copy-start.2 = (u32[32]{0:T(128)S(1)}, u32[32]{0:T(128)}, u32[]{:S(2)}) copy-start(u32[32]{0:T(128)} %constant.70) | copy-start | bytes 388
  70.3 10.1 %all-to-all-start.2 = ((bf16[64,1,48]{2,1,0:T(2,128)(2,1)}), bf16[64,1,48]{2,1,0:T(2,128)(2,1)S(1)}, u32[]{:S(2)}, u32[]{:S(2)}) async-start(bf16[64,1,48]{2,1,0:T(2,128)(2,1)} %copy.39), calls=%async_computation.2 | async-start | bytes 65536 | tf_op jit(solution)/shard_map/all_to_all | solution.py:52
  89.6 54.9 %all-to-all-start.1 = ((bf16[64,1,48,128]{3,2,1,0:T(8,128)(2,1)}), bf16[64,1,48,128]{3,2,1,0:T(8,128)(2,1)S(1)}, u32[]{:S(2)}, u32[]{:S(2)}) async-start(bf16[64,1,48,128]{3,2,1,0:T(8,128)(2,1)} %bitcast.20), calls=%async_computation.1 | async-start | bytes 1572864 | tf_op jit(solution)/shard_map/all_to_all | solution.py:46
where the time goes:
time: 217 us; the launch traced here: 215 us
  blocking collectives  151 us (70%)
  matrix products  30.3 us (14%)
  local copies, waits for them, and re-layouts  16.7 us (8%)
  starting transfers between devices  7.11 us (3%)
  waiting for transfers between devices  6.56 us (3%)
  other arithmetic  2.41 us (1%)
    unnamed x1, blocking collectives  66.3 us
    all_gather x1, blocking collectives, on_device(): lax.all_gather(levels, 'seq', axis=1, tiled=True)  29.1 us
    all_gather x1, blocking collectives, on_device(): gathered = lax.all_gather(queries, 'seq', axis=0, tiled=True)  26.4 us
    all_gather x1, blocking collectives, on_device(): lax.all_gather(owner_map, 'seq', axis=1, tiled=True)  20.1 us
    dot_general x8, matrix products, local_block(): jnp.einsum('pqk,kph->pqh', expo.astype(jnp.bfloat16), value_block, prefer...  16.2 us
    unnamed x17, local copies, waits for them, and re-layouts  13.8 us
    dot_general x8, matrix products, local_block(): jnp.einsum('qph,kph->pqk', query_block, key_block, preferred_element_type...  10.7 us
    all_to_all x1, blocking collectives, on_device(): lax.all_to_all(peak[:, None].astype(jnp.bfloat16), 'seq', split_axis=0, c...  9.19 us
  transfers between devices with their start and end apart: 2, of which 1 were waited for; matrix products, arithmetic and copies ran while one was open for 1% of the time, Pallas kernels for 0%

commit v1 on v0

v1 whole, which is shorter than its diff:
```python
import functools

import jax
import jax.numpy as jnp
from jax import lax
from jax.experimental import pallas as pl
from jax.experimental.pallas import tpu as pltpu
from jax.sharding import PartitionSpec as P

HD = 128
HEADS = 16
CONTROLS = 3
LEVELS = 8
LANES = 128
BASE = 256

VMEM = pl.BlockSpec(memory_space=pltpu.VMEM)


def rows_of(tokens, heads_dev):
    tiles = -(-tokens // LANES)
    return heads_dev * tokens, tiles, -(-(2 * heads_dev * tiles) // 8) * 8


def attend_kernel(tokens, heads_dev, q_ref, k_ref, v_ref, out_ref, stat_ref):
    pairs = k_ref.shape[1] // HD
    main, tiles, _ = rows_of(tokens, heads_dev)
    group = max(4, heads_dev)
    lane = lax.broadcasted_iota(jnp.int32, (tokens, LANES), 1)
    stat_ref[...] = jnp.zeros_like(stat_ref)

    def step(g, carry):
        stat = stat_ref[:tokens, :]
        for first in range(0, group, 2):
            expo = []
            for j in (first, first + 1):
                head = g * group + j
                columns = pl.ds(pl.multiple_of(head * HD, HD), HD)
                scores = lax.dot_general(
                    q_ref[:, columns], k_ref[:, columns], (((1,), (1,)), ((), ())), preferred_element_type=jnp.float32
                ) * HD ** (-0.5)
                peak = jnp.max(scores, axis=1, keepdims=True).astype(jnp.bfloat16).astype(jnp.float32)
                weights = jnp.exp(scores - peak)
                total = jnp.sum(weights, axis=1, keepdims=True)
                expo.append(weights.astype(jnp.bfloat16))
                place = (g * (group // heads_dev) + j // heads_dev) * 2 * heads_dev + j % heads_dev
                stat = jnp.where(lane == place, peak, jnp.where(lane == place + heads_dev, total, stat))
            both = pl.ds(pl.multiple_of((g * group + first) * HD, 2 * HD), 2 * HD)
            product = jnp.dot(jnp.concatenate(expo, axis=0), v_ref[:, both], preferred_element_type=jnp.float32)
            for i, j in enumerate((first, first + 1)):
                row = (j % heads_dev) * tokens
                out_ref[g * (group // heads_dev) + j // heads_dev, row : row + tokens, :] = product[
                    i * tokens : (i + 1) * tokens, i * HD : (i + 1) * HD
                ].astype(jnp.bfloat16)
        stat_ref[:tokens, :] = stat
        return carry

    lax.fori_loop(0, pairs // group, step, 0, unroll=2)
    for tile in range(tiles):
        turned = stat_ref[tile * LANES : (tile + 1) * LANES, :].T.astype(jnp.bfloat16)
        for device in range(pairs // heads_dev):
            at = main + tile * 2 * heads_dev
            out_ref[device, at : at + 2 * heads_dev, :] = turned[device * 2 * heads_dev : (device + 1) * 2 * heads_dev, :]


def project_kernel(tokens, heads_dev, x_ref, w_ref, meta_ref, out_ref):
    count = x_ref.shape[0]
    main, tiles, _ = rows_of(tokens, heads_dev)
    span = 2 * heads_dev
    shares = []
    for tile in range(tiles):
        at = main + tile * span
        rows = jnp.concatenate([x_ref[i, at : at + span, :].astype(jnp.float32) for i in range(count)], axis=0)
        stat = rows.T
        best, shift = stat, span
        while shift < LANES:
            best = jnp.maximum(best, pltpu.roll(best, shift, 1))
            shift *= 2
        factor = jnp.exp(stat - best)
        denom, shift = factor * pltpu.roll(stat, LANES - heads_dev, 1), span
        while shift < LANES:
            denom = denom + pltpu.roll(denom, shift, 1)
            shift *= 2
        shares.append(factor / denom)
    share = jnp.concatenate(shares, axis=0)[:tokens, :]
    attended = []
    for h in range(heads_dev):
        total = jnp.zeros((tokens, HD), jnp.float32)
        for i in range(count):
            part = x_ref[i, h * tokens : (h + 1) * tokens, :].astype(jnp.float32)
            total = total + share[:, i * span + h : i * span + h + 1] * part
        attended.append(total.astype(jnp.bfloat16))
    attended = jnp.concatenate(attended, axis=1)

    section = lax.axis_index("seq") * heads_dev // HEADS
    control = jnp.minimum(section, CONTROLS - 1)
    is_base = section >= CONTROLS
    meta = meta_ref[...].astype(jnp.float32)
    lane = lax.broadcasted_iota(jnp.int32, meta.shape, 1)

    def column(index):
        return jnp.sum(jnp.where(lane == index, meta, 0.0), axis=1, keepdims=True)

    owner = column(CONTROLS + control) + BASE * column(2 * CONTROLS + control)
    level = column(control)
    token = lax.broadcasted_iota(jnp.int32, (tokens, 1), 0).astype(jnp.float32)
    owner = jnp.where(is_base, token, owner)
    level = jnp.where(is_base, float(LEVELS), level)
    places = lax.broadcasted_iota(jnp.int32, (tokens, tokens), 1).astype(jnp.float32)
    selector = (owner == places).astype(jnp.bfloat16)
    turn = (((0,), (0,)), ((), ()))
    mixed = lax.dot_general(selector, attended, turn, preferred_element_type=jnp.float32).astype(jnp.bfloat16)
    wide = jnp.broadcast_to(level, (tokens, LANES)).astype(jnp.bfloat16)
    weight = lax.dot_general(selector, wide, turn, preferred_element_type=jnp.float32)[:, :1] / LEVELS
    width = 512
    for at in range(0, w_ref.shape[1], width):
        out_ref[:, at : at + width] = (
            jnp.dot(mixed, w_ref[:, at : at + width], preferred_element_type=jnp.float32) * weight
        ).astype(jnp.bfloat16)


def on_device(queries, key_rows, value_rows, out_weight, levels, owner_map):
    count = lax.axis_size("seq")
    tokens = queries.shape[0] * count
    pairs = queries.shape[1] // HD
    heads_dev = out_weight.shape[0] // HD
    main, tiles, extra = rows_of(tokens, heads_dev)
    meta = jnp.concatenate([levels, owner_map % BASE, owner_map // BASE], axis=0).T.astype(jnp.bfloat16)
    meta = jnp.pad(meta, ((0, 0), (0, LANES - meta.shape[1])))
    gathered = lax.all_gather(jnp.concatenate([queries, meta], axis=1), "seq", axis=0, tiled=True)
    parts = pl.pallas_call(
        functools.partial(attend_kernel, tokens, heads_dev),
        out_shape=jax.ShapeDtypeStruct((count, main + extra, HD), jnp.bfloat16),
        in_specs=[VMEM] * 3,
        out_specs=VMEM,
        scratch_shapes=[pltpu.VMEM((tiles * LANES, LANES), jnp.float32)],
        name="attend",
    )(gathered, key_rows, value_rows)
    parts = lax.all_to_all(parts, "seq", split_axis=0, concat_axis=0, tiled=True)
    projected = pl.pallas_call(
        functools.partial(project_kernel, tokens, heads_dev),
        out_shape=jax.ShapeDtypeStruct((tokens, out_weight.shape[1]), jnp.bfloat16),
        in_specs=[VMEM] * 3,
        out_specs=VMEM,
        name="project",
    )(parts, out_weight, gathered[:, pairs * HD :])
    summed = lax.all_to_all(
        projected.reshape(count, tokens // count, -1), "seq", split_axis=0, concat_axis=0, tiled=True
    )
    return jnp.sum(summed.astype(jnp.float32), axis=0).astype(jnp.bfloat16)


def solution(mesh):
    return jax.shard_map(
        on_device,
        mesh=mesh,
        in_specs=(
            P(("groups", "seq"), None),
            P(("groups", "seq"), None),
            P(("groups", "seq"), None),
            P("seq", None),
            P(None, ("groups", "seq")),
            P(None, ("groups", "seq")),
        ),
        out_specs=P(("groups", "seq"), None),
        check_vma=False,
    )
```

time: 217 us -> 94.4 us (0.44)
  blocking collectives: 151 us -> 45.8 us
  matrix products: 30.3 us -> 0 us
  Pallas kernels: 0 us -> 18.5 us
  waiting for transfers between devices: 6.56 us -> 17.9 us
  local copies, waits for them, and re-layouts: 16.7 us -> 6.42 us
  starting transfers between devices: 7.11 us -> 3.62 us
    unnamed x1 -> x0, blocking collectives: 66.3 us -> none
    all_gather x3 -> x1, blocking collectives: 75.6 us -> 26.2 us  [on_device(): lax.all_gather(jnp.concatenate([queries, meta], axis=1), 'seq', axis=0, t...]
    dot_general x19 -> x0, matrix products: 30.3 us -> none  [the longest x8 16.2 us: local_block(): jnp.einsum('pqk,kph->pqh', expo.astype(jnp.bfloat16), value_block, prefer...]
    pallas_call x0 -> x2, Pallas kernels: none -> 18.5 us  [the longest x1 13.1 us: on_device(): pl.pallas_call(functools.partial(attend_kernel, tokens, heads_dev), out_s...]
    all_to_all x2 -> x1, waiting for transfers between devices: 6.56 us -> 17.9 us  [on_device(): lax.all_to_all(parts, 'seq', split_axis=0, concat_axis=0, tiled=True)]
    all_to_all x1, blocking collectives: 9.19 us -> 19.6 us  [on_device(): lax.all_to_all(projected.reshape(count, tokens // count, -1), 'seq', spli...]
    unnamed x17 -> x5, local copies, waits for them, and re-layouts: 13.8 us -> 3.89 us
    all_to_all x2 -> x1, starting transfers between devices: 7.11 us -> 3.62 us  [on_device(): lax.all_to_all(parts, 'seq', split_axis=0, concat_axis=0, tiled=True)]
  transfers between devices with their start and end apart: 2 -> 1, of which waited for: 1 -> 1; matrix products, arithmetic and copies ran while one was open for 1% -> 1% of each run, Pallas kernels for 0% -> 0%
where the time goes in v1:
time: 94.4 us; the launch traced here: 94 us
  blocking collectives  45.8 us (49%)
  Pallas kernels  18.5 us (20%)
  waiting for transfers between devices  17.9 us (19%)
  local copies, waits for them, and re-layouts  6.42 us (7%)
  starting transfers between devices  3.62 us (4%)
  other arithmetic  1.81 us (2%)
    all_gather x1, blocking collectives, on_device(): lax.all_gather(jnp.concatenate([queries, meta], axis=1), 'seq', axis=0, t...  26.2 us
    all_to_all x1, blocking collectives, on_device(): lax.all_to_all(projected.reshape(count, tokens // count, -1), 'seq', spli...  19.6 us
    all_to_all x1, waiting for transfers between devices, on_device(): lax.all_to_all(parts, 'seq', split_axis=0, concat_axis=0, tiled=True)  17.9 us
    pallas_call x1, Pallas kernels, on_device(): pl.pallas_call(functools.partial(attend_kernel, tokens, heads_dev), out_s...  13.1 us
    pallas_call x1, Pallas kernels, on_device(): pl.pallas_call(functools.partial(project_kernel, tokens, heads_dev), out_...  5.42 us
    unnamed x5, local copies, waits for them, and re-layouts  3.89 us
    all_to_all x1, starting transfers between devices, on_device(): lax.all_to_all(parts, 'seq', split_axis=0, concat_axis=0, tiled=True)  3.62 us
  transfers between devices with their start and end apart: 1, of which 1 were waited for; matrix products, arithmetic and copies ran while one was open for 1% of the time, Pallas kernels for 0%

profile of v1, /device:TPU:0, one launch (start us, length us, event | category | flops | bytes accessed | tf_op | source)
XLA Modules:
  0.0 94.0 jit_solution(10662920736992780904)
XLA Ops:
  0.0 0.8 copy.9
  0.8 0.8 copy.10
  1.6 0.1 maximum_bitcast_fusion
  1.6 0.9 fusion.2
  2.5 26.2 %all-gather = bf16[16,3,8320]{2,1,0:T(4,128)(2,1)S(1)} all-gather(bf16[1,3,8320]{2,1,0:T(4,128)(2,1)S(1)} %fusion.2), channel_id=1, replica_groups=mesh['groups'=2,'seq'=16] {'seq'}, dimensions={0}, use_global_device_ids=true | all-gather | bytes 848640 | tf_op jit(solution)/shard_map/all_gather | solution.py:130
  28.7 1.5 %reshape.5.q_ref = bf16[48,8320]{1,0:T(8,128)(2,1)} reshape(bf16[16,3,8320]{2,1,0:T(4,128)(2,1)S(1)} %all-gather) | data formatting | bytes 1597440
  30.2 13.1 %attend.1 = bf16[16,200,128]{2,1,0:T(8,128)(2,1)} custom-call(bf16[48,8320]{1,0:T(8,128)(2,1)} %reshape.5.q_ref, bf16[256,8192]{1,0:T(8,128)(2,1)} %k_ref.1, bf16[256,8192]{1,0:T(8,128)(2,1)} %v_ref.1), custom_call_target="tpu_custom_call" | custom-call | tf_op jit(solution)/shard_map/attend/pallas_call | solution.py:131
  43.2 3.6 %all-to-all-start = ((bf16[16,200,128]{2,1,0:T(8,128)(2,1)}), bf16[16,200,128]{2,1,0:T(8,128)(2,1)S(1)}, u32[]{:S(2)}, u32[]{:S(2)}) async-start(bf16[16,200,128]{2,1,0:T(8,128)(2,1)} %attend.1), calls=%async_computation | async-start | bytes 1638400 | tf_op jit(solution)/shard_map/all_to_all | solution.py:139
  46.9 1.3 %slice.4.meta_ref = bf16[48,128]{1,0:T(8,128)(2,1)} slice(bf16[48,8320]{1,0:T(8,128)(2,1)} %reshape.5.q_ref), slice={[0:48], [8192:8320]} | slice | bytes 24576 | tf_op jit(solution)/shard_map/slice | solution.py:146
  48.2 17.9 %all-to-all-done.x_ref = bf16[16,200,128]{2,1,0:T(8,128)(2,1)S(1)} async-done(((bf16[16,200,128]{2,1,0:T(8,128)(2,1)}), bf16[16,200,128]{2,1,0:T(8,128)(2,1)S(1)}, u32[]{:S(2)}, u32[]{:S(2)}) %all-to-all-start) | async-done | bytes 819232 | tf_op jit(solution)/shard_map/all_to_all | solution.py:139
  66.0 0.0 copy-start
  66.0 0.9 copy-done
  66.9 5.4 %project.1 = bf16[48,4096]{1,0:T(8,128)(2,1)} custom-call(bf16[16,200,128]{2,1,0:T(8,128)(2,1)} %copy-done, bf16[512,4096]{1,0:T(8,128)(2,1)} %w_ref.1, bf16[48,128]{1,0:T(8,128)(2,1)} %slice.4.meta_ref), custom_call_target="tpu_custom_call" | custom-call | tf_op jit(solution)/shard_map/project/pallas_call | solution.py:140
  72.4 1.2 %reshape.3 = bf16[16,3,4096]{2,1,0:T(4,128)(2,1)S(1)} reshape(bf16[48,4096]{1,0:T(8,128)(2,1)} %project.1) | data formatting | bytes 786432 | tf_op jit(solution)/shard_map/reshape | solution.py:148
  73.6 19.6 %all_to_all.10 = bf16[16,3,4096]{2,1,0:T(4,128)(2,1)S(1)} all-to-all(bf16[16,3,4096]{2,1,0:T(4,128)(2,1)S(1)} %reshape.3), channel_id=1, replica_groups=mesh['groups'=2,'seq'=16] {'seq'}, dimensions={0} | all-to-all | bytes 786432 | tf_op jit(solution)/shard_map/all_to_all | solution.py:147
  93.2 0.8 reduce_sum.12
  (2 shorter events, 0.0 us)
Async XLA Ops:
  43.2 22.8 %all-to-all-start = ((bf16[16,200,128]{2,1,0:T(8,128)(2,1)}), bf16[16,200,128]{2,1,0:T(8,128)(2,1)S(1)}, u32[]{:S(2)}, u32[]{:S(2)}) async-start(bf16[16,200,128]{2,1,0:T(8,128)(2,1)} %attend.1), calls=%async_computation | async-start | bytes 1638400 | tf_op jit(solution)/shard_map/all_to_all | solution.py:139
  66.0 0.9 copy-start
